TPU v7x, 256 devices: a whole 4x4x8 slice. The times are simulated.
256 devices in a mesh: cluster: 16 (over y_hi, z), client: 16 (over x, y_lo, core).
Axes of the slice: x: 4, y: 4 (y_hi: 2, y_lo: 2; y = y_hi * 2 + y_lo), z: 8, core: 2. Of those that a mesh axis runs over, the one named last changes fastest.
Arguments:
- user_feats: bfloat16 [24576, 2048], P('client'), may hold values from -6 to 6
- item_feats: bfloat16 [24576, 2048], P('client'), may hold values from -6 to 6
- item_ids: int32 [24576], P('client'), may hold values from 0 to 999
- picks: int32 [256], P('client'), may hold values from 0 to 15
- user_weight: bfloat16 [16, 2048, 512], P('cluster'), may hold values from -0.125 to 0.125
- item_weight: bfloat16 [16, 2048, 512], P('cluster'), may hold values from -0.125 to 0.125
Outputs:
- loss_table: float32 [256, 16], P('client')
- user_grad: float32 [16, 2048, 512], P('cluster', 'client')
- item_grad: float32 [16, 2048, 512], P('cluster', 'client')
Inputs may be any that keep to these rules, and one draw needn't show every extreme that they name: `picks`: one cluster per client.
All inputs are finite; a program needn't handle non-finite values.
Results may differ from a plain program's by a relative error of at most 0.005.
Values sent between devices are 32-bit elements; how exact they have to be, the bound alone decides.
A program may use at most 128 MiB of HBM per device.

v0:
```python
import functools
import math

import jax
import jax.numpy as jnp
from jax import lax
from jax.experimental import pallas as pl
from jax.experimental.pallas import tpu as pltpu
from jax.sharding import PartitionSpec as P

MESH = pl.DeviceIdType.MESH
NX = 4
ORDER = (2, 1, 3, 0)
PAIR = 2
PICKED_BYTES = 24 * 1024 * 1024
ROUND_BYTES = 46 * 1024 * 1024
FINISH_BYTES = 8 * 1024 * 1024
F32, BF16 = jnp.float32, jnp.bfloat16


def dot(a, b, dims=((1,), (0,))):
    return lax.dot_general(a, b, (dims, ((), ())), preferred_element_type=F32)


def same_item(ids, first, off, rows):
    shape = (rows, 128)
    last = ids.shape[0] - 1
    back = (128 - off) % 128
    got = pltpu.roll(jnp.broadcast_to(ids[pl.ds(first, 1), :], shape), back, 1)
    more = pltpu.roll(jnp.broadcast_to(ids[pl.ds(jnp.minimum(first + 1, last), 1), :], shape), back, 1)
    got = jnp.where(lax.broadcasted_iota(jnp.int32, shape, 1) < 128 - off, got, more)[:, :rows]
    return got == got.T


def columns(s_me, step):
    q = step // 2
    dx = (2 + 3 * q + 3 * (q * (q - 1) // 2)) % NX
    dy = 1 - step % 2
    chip = ((s_me // 4 + dx) % NX) * 2 + ((s_me // 2) % 2 + dy) % 2
    return pl.ds(pl.multiple_of(chip * 256, 256), 256)


def picked(cfg, uf, itf, ids_hbm, picks_hbm, uw, iw, us_out, is_out, cu_out, ci_out,
           ids, picks, chosen, wu, wi, bu, bi, dsilu, uvec, iv, sem, bsem):
    clients, rows, width = cfg
    temper = 1.0 / math.sqrt(width)
    k_me = lax.axis_index("cluster")
    loads = [pltpu.make_async_copy(src, dst, sem.at[n]) for n, (src, dst) in enumerate(
        ((picks_hbm, picks), (uw.at[0], wu), (iw.at[0], wi), (ids_hbm, ids)))]
    for copy in loads:
        copy.start()
    loads[0].wait()

    def scan(client, count):
        chosen[count] = client
        return count + jnp.where(picks[client] == k_me, 1, 0)

    count = lax.fori_loop(0, clients, scan, 0)

    @pl.when(count % PAIR == 1)
    def _():
        chosen[count] = chosen[count - 1]

    pairs = (count + 1) // PAIR

    def fetch(p):
        slot = p % 2
        copies = []
        for n in range(PAIR):
            at = pl.ds(pl.multiple_of(chosen[PAIR * p + n] * rows, rows), rows)
            to = pl.ds(n * rows, rows)
            copies.append(pltpu.make_async_copy(uf.at[at], bu.at[slot, to], bsem.at[slot, 0, n]))
            copies.append(pltpu.make_async_copy(itf.at[at], bi.at[slot, to], bsem.at[slot, 1, n]))
        return copies

    @pl.when(pairs > 0)
    def _():
        for copy in fetch(0):
            copy.start()

    def clear(n, carry):
        at = pl.ds(pl.multiple_of(n * 64, 64), 64)
        us_out[at, :] = jnp.zeros((64, width), BF16)
        is_out[at, :] = jnp.zeros((64, width), BF16)
        return carry

    first = columns(lax.axis_index("client"), 0)
    ahead = [pltpu.make_async_copy(src.at[:, first], dst, sem.at[4 + t])
             for t, (src, dst) in enumerate(((uf, cu_out), (itf, ci_out)))]
    for copy in ahead:
        copy.start()
    lax.fori_loop(0, clients * rows // 64, clear, 0)
    for copy in loads[1:]:
        copy.wait()

    def pair(p, carry):
        slot = p % 2

        @pl.when(p + 1 < pairs)
        def _():
            for copy in fetch(p + 1):
                copy.start()

        for copy in fetch(p):
            copy.wait()
        pre = dot(bu[slot], wu[...])
        sig = 0.5 * jnp.tanh(0.5 * pre) + 0.5
        u = pre * sig
        uvec[...] = u.astype(BF16)
        dsilu[...] = sig + (u - u * sig)
        iv[...] = dot(bi[slot], wi[...]).astype(BF16)
        for n in range(PAIR):
            client = chosen[PAIR * p + n]
            at = slice(n * rows, (n + 1) * rows)
            u = uvec[at, :]
            v = iv[at, :]
            s = dot(u, v, ((1,), (1,))) * temper
            start = client * rows
            same = same_item(ids, start // 128, start % 128, rows)
            gate = 0.5 * jnp.tanh(0.5 * s) + 0.5
            slope = (jnp.where(same, gate - 1.0, gate) * temper).astype(BF16)
            to = pl.ds(pl.multiple_of(start, rows), rows)
            us_out[to, :] = (dot(slope, v) * dsilu[at, :]).astype(BF16)
            is_out[to, :] = dot(slope, u, ((0,), (0,))).astype(BF16)
        return carry

    lax.fori_loop(0, pairs, pair, 0)
    for copy in ahead:
        copy.wait()


def kernel(cfg, uf, itf, ids_hbm, uw, iw, us, its, cu, ci, fin, table,
           ids, fu, fi, wu, wi, iv, uvec, gt, crecv, ya, yb,
           xa1, xal, xar, xb1, xbl, xbr,
           ld, cs, cr, ys, yr, xs, xr, ls, lr):
    clients, rows, width, split, groups, clusters = cfg
    total, depth = fu.shape
    per = clients // groups
    grp = per * rows
    temper = 1.0 / math.sqrt(width)
    k_me = lax.axis_index("cluster")
    s_me = lax.axis_index("client")
    x = s_me // 4
    y = (s_me // 2) % 2
    c = s_me % 2
    mate = {"client": x * 4 + y * 2 + (1 - c)}
    across = {"client": x * 4 + (1 - y) * 2 + c}
    right = {"client": ((x + 1) % NX) * 4 + y * 2 + c}
    left = {"client": ((x + NX - 1) % NX) * 4 + y * 2 + c}
    nz = clusters // 2
    h = k_me // nz
    z = k_me % nz
    twin = {"cluster": (1 - h) * nz + z}
    above = {"cluster": h * nz + (z + 1) % nz}
    below = {"cluster": h * nz + (z + nz - 1) % nz}

    barrier = pltpu.get_barrier_semaphore()
    for peer in (mate, across, right, left, twin, above, below):
        pl.semaphore_signal(barrier, inc=1, device_id=peer, device_id_type=MESH)

    def feats(step, t):
        src, dst = ((uf, fu), (itf, fi))[t]
        at = columns(s_me, step)
        return pltpu.make_async_copy(src.at[:, at], dst.at[:, at], ld.at[step, t])

    rest_loads = [pltpu.make_async_copy(src, dst, ld.at[2 * NX, n]) for n, (src, dst) in enumerate(
        ((uw.at[0], wu), (iw.at[0], wi), (ids_hbm, ids)))]
    for step in (1, 2):
        for t in (0, 1):
            feats(step, t).start()

    A = pl.ds(0, split)
    B = pl.ds(split, 128 - split)

    def step_of(dx, dy):
        return 2 * ORDER.index(dx) + (1 - dy)

    def own(dx, dy, t, part):
        return gt.at[step_of(dx, dy), t, c, part]

    def send(src, dst, ssem, rsem, peer):
        return pltpu.make_async_remote_copy(src_ref=src, dst_ref=dst, send_sem=ssem, recv_sem=rsem,
                                            device_id=peer, device_id_type=MESH)

    def twin_copy():
        return send(table.at[h, z], table.at[h, z], ls.at[0], lr.at[0], twin)

    def loss_copy(n, up):
        part = table.at[:, pl.ds((z + (nz - n if up else n)) % nz, 1)]
        sem = 1 + 2 * n + (0 if up else 1)
        return send(part, part, ls.at[sem], lr.at[sem], above if up else below)

    def loss_copies(n):
        return [loss_copy(n, True)] + ([loss_copy(n, False)] if n < nz // 2 - 1 else [])

    def loss_step(n):
        if n == 0:
            twin_copy().wait_recv()
        else:
            for copy in loss_copies(n - 1):
                copy.wait_recv()
        if n < nz // 2:
            for copy in loss_copies(n):
                copy.start()

    def core_copy(step, t):
        return send(gt.at[step, t, 1 - c], crecv.at[step, t], cs.at[step, t], cr.at[step, t], mate)

    def ya_copy(dx, t):
        return send(own(dx, 1, t, A), ya.at[dx, t], ys.at[dx, t], yr.at[dx, t], across)

    def yb_copy(t):
        return send(own(0, 1, t, B), yb.at[t], ys.at[4, t], yr.at[4, t], across)

    def x_part(which):
        return (0, A, xa1, xal, xar) if which == 2 else (which, B, xb1.at[which], xbl.at[which], xbr.at[which])

    def far_copy(which, t):
        dy, part, first, _, _ = x_part(which)
        return send(own(2, dy, t, part), first.at[t], xs.at[which, 0, t], xr.at[which, 0, t], (right, left)[t])

    def near_copy(which, t, rightward):
        dy, part, _, from_left, from_right = x_part(which)
        if rightward:
            return send(own(1, dy, t, part), from_left.at[t], xs.at[which, 1, t], xr.at[which, 1, t], right)
        return send(own(3, dy, t, part), from_right.at[t], xs.at[which, 2, t], xr.at[which, 2, t], left)

    def add(dst, src):
        dst[...] += src[...]

    def far_arrived(which, t):
        dy, part, first, _, _ = x_part(which)
        far_copy(which, t).wait_recv()
        add(own((1, 3)[t], dy, t, part), first.at[t])
        near_copy(which, t, t == 0).start()

    def near_arrived(which):
        dy, part, _, from_left, from_right = x_part(which)
        for t in (0, 1):
            near_copy(which, t, True).wait_recv()
            near_copy(which, t, False).wait_recv()
            mine = own(0, dy, t, part)
            mine[...] += from_left[t] + from_right[t]

    def ya_arrived(dx):
        for t in (0, 1):
            ya_copy(dx, t).wait_recv()
            add(own(dx, 0, t, A), ya.at[dx, t])

    def ready(step):
        dx, dy = ORDER[step // 2], 1 - step % 2
        for t in (0, 1):
            core_copy(step, t).wait_recv()
            mine = gt.at[step, t, c]
            mine[...] += crecv[step, t]
            if dx == 2:
                far_copy(dy, t).start()
            if dy == 1:
                ya_copy(dx, t).start()
            if dx == 1 and t == 1:
                near_copy(dy, 1, True).start()
            if dx == 3 and t == 0:
                near_copy(dy, 0, False).start()

    def block(step, lhs):
        for t, (slope, feat) in enumerate(((us, lhs[0]), (its, lhs[1]))):
            r = dot(feat(), slope[...], ((0,), (0,)))
            gt[step, t, 0] = r[:128]
            gt[step, t, 1] = r[128:]
            if isinstance(step, int) and step == 0 and t == 0:
                pl.semaphore_wait(barrier, 7)
            core_copy(step, t).start()

    def loaded(step):
        def of(t, buf):
            feats(step, t).wait()
            return buf[:, columns(s_me, step)]
        return functools.partial(of, 0, fu), functools.partial(of, 1, fi)

    def blocks(step, carry):
        @pl.when(step + 2 < 2 * NX)
        def _():
            for t in (0, 1):
                feats(step + 2, t).start()

        @pl.when(step == 2 * NX - 3)
        def _():
            for copy in rest_loads:
                copy.start()
            for t in (0, 1):
                feats(0, t).start()

        block(step, loaded(step))
        for n in range(2 * NX - 2):
            @pl.when(step == n + 1)
            def _(n=n):
                ready(n)
                if n == 5:
                    far_arrived(1, 0)
                    far_arrived(1, 1)
        return carry

    block(0, (lambda: cu[...], lambda: ci[...]))
    lax.fori_loop(1, 2 * NX - 1, blocks, 0)
    ready(2 * NX - 2)
    far_arrived(0, 0)
    far_arrived(0, 1)
    for copy in rest_loads:
        copy.wait()
    for t in (0, 1):
        feats(0, t).wait()
        feats(2 * NX - 1, t).wait()

    lane = lax.broadcasted_iota(jnp.int32, (1, 128), 1)

    def losses_of(g, losses):
        at = pl.ds(pl.multiple_of(g * grp, grp), grp)
        pre = dot(fu[at, :], wu[...])
        uvec[...] = (pre * (0.5 * jnp.tanh(0.5 * pre) + 0.5)).astype(BF16)
        iv[...] = dot(fi[at, :], wi[...]).astype(BF16)
        for n in range(per):
            rows_n = slice(n * rows, (n + 1) * rows)
            s = dot(uvec[rows_n, :], iv[rows_n, :], ((1,), (1,))) * temper
            first, off = divmod(n * rows, 128)
            same = same_item(ids, g * (grp // 128) + first, off, rows)
            pair = jnp.maximum(s, 0.0) + jnp.log(1.0 + jnp.exp(-jnp.abs(s))) - jnp.where(same, s, 0.0)
            mean = jnp.sum(pair, axis=(0, 1), keepdims=True) * (1.0 / (rows * rows))
            losses = jnp.where(lane == g * per + n, mean, losses)

        @pl.when(g == 0)
        def _():
            ya_arrived(2)
            far_copy(2, 0).start()
            far_copy(2, 1).start()

        @pl.when(g == 1)
        def _():
            ya_arrived(1)
            near_copy(2, 1, True).start()

        return losses

    losses = lax.fori_loop(0, groups, losses_of, jnp.zeros((1, 128), F32))
    table[h, z] = losses
    twin_copy().start()
    block(2 * NX - 1, (lambda: fu[:, columns(s_me, 2 * NX - 1)], lambda: fi[:, columns(s_me, 2 * NX - 1)]))
    ya_arrived(3)
    near_copy(2, 0, False).start()
    loss_step(0)
    near_arrived(1)
    yb_copy(0).start()
    yb_copy(1).start()
    ready(2 * NX - 1)
    loss_step(1)
    far_arrived(2, 0)
    far_arrived(2, 1)
    near_arrived(0)
    ya_arrived(0)
    loss_step(2)
    loss_step(3)
    for t in (0, 1):
        yb_copy(t).wait_recv()
        fin[t, split:, :] = gt[step_of(0, 0), t, c, split:, :] + yb[t]
    for t in (0, 1):
        near_copy(2, t, True).wait_recv()
        near_copy(2, t, False).wait_recv()
        fin[t, :split, :] = gt[step_of(0, 0), t, c, :split, :] + xal[t] + xar[t]
    loss_step(4)

    twin_copy().wait_send()
    for n in range(nz // 2):
        for copy in loss_copies(n):
            copy.wait_send()
    for step in range(2 * NX):
        for t in (0, 1):
            core_copy(step, t).wait_send()
    for t in (0, 1):
        for dx in range(NX):
            ya_copy(dx, t).wait_send()
        yb_copy(t).wait_send()
        for which in range(3):
            far_copy(which, t).wait_send()
            near_copy(which, t, True).wait_send()
            near_copy(which, t, False).wait_send()


def finish(fin, table, loss_out, ug_out, ig_out):
    clients, clusters = loss_out.shape
    ug_out[0] = fin[0]
    ig_out[0] = fin[1]
    loss_out[...] = table[...].reshape(clusters, 128).T[:clients, :]


def body(user_feats, item_feats, item_ids, picks, user_weight, item_weight):
    clients = picks.shape[0]
    total, depth = user_feats.shape
    rows = total // clients
    width = user_weight.shape[2]
    clusters = lax.axis_size("cluster")
    groups = 4
    grp = total // groups
    split = 56
    rest = 128 - split
    vmem = pltpu.VMEM
    dma = pltpu.SemaphoreType.DMA
    hbm_spec = pl.BlockSpec(memory_space=pltpu.HBM)
    vmem_spec = pl.BlockSpec(memory_space=pltpu.VMEM)
    uf, itf, ids, picks, uw, iw = [pltpu.with_memory_space_constraint(a, pltpu.HBM) for a in (
        user_feats, item_feats, item_ids.reshape(total // 128, 128), picks, user_weight, item_weight)]
    us, its, cu, ci = pl.pallas_call(
        functools.partial(picked, (clients, rows, width)),
        out_shape=tuple(jax.ShapeDtypeStruct((total, n), BF16) for n in (width, width, 256, 256)),
        in_specs=[hbm_spec] * 6,
        out_specs=(vmem_spec,) * 4,
        scratch_shapes=[
            vmem((total // 128, 128), jnp.int32), pltpu.SMEM((clients,), jnp.int32), pltpu.SMEM((clients,), jnp.int32),
            vmem((depth, width), BF16), vmem((depth, width), BF16),
            vmem((2, PAIR * rows, depth), BF16), vmem((2, PAIR * rows, depth), BF16),
            vmem((PAIR * rows, width), F32), vmem((PAIR * rows, width), BF16), vmem((PAIR * rows, width), BF16),
            dma((6,)), dma((2, 2, PAIR)),
        ],
        compiler_params=pltpu.CompilerParams(vmem_limit_bytes=PICKED_BYTES),
        name="picked",
    )(uf, itf, ids, picks, uw, iw)
    fin, table = pl.pallas_call(
        functools.partial(kernel, (clients, rows, width, split, groups, clusters)),
        out_shape=(jax.ShapeDtypeStruct((2, 128, width), F32), jax.ShapeDtypeStruct((2, clusters // 2, 1, 128), F32)),
        in_specs=[hbm_spec] * 5 + [vmem_spec] * 4,
        out_specs=(vmem_spec, vmem_spec),
        scratch_shapes=[
            vmem((total // 128, 128), jnp.int32),
            vmem((total, depth), BF16), vmem((total, depth), BF16),
            vmem((depth, width), BF16), vmem((depth, width), BF16),
            vmem((grp, width), BF16), vmem((grp, width), BF16),
            vmem((8, 2, 2, 128, width), F32), vmem((8, 2, 128, width), F32),
            vmem((4, 2, split, width), F32), vmem((2, rest, width), F32),
            vmem((2, split, width), F32), vmem((2, split, width), F32), vmem((2, split, width), F32),
            vmem((2, 2, rest, width), F32), vmem((2, 2, rest, width), F32), vmem((2, 2, rest, width), F32),
            dma((2 * NX + 1, 3)), dma((8, 2)), dma((8, 2)), dma((5, 2)), dma((5, 2)),
            dma((3, 3, 2)), dma((3, 3, 2)), dma((clusters,)), dma((clusters,)),
        ],
        compiler_params=pltpu.CompilerParams(
            collective_id=0, has_side_effects=True, vmem_limit_bytes=ROUND_BYTES),
        name="round",
    )(uf, itf, ids, uw, iw, us, its, cu, ci)
    return pl.pallas_call(
        finish,
        out_shape=(
            jax.ShapeDtypeStruct((clients, clusters), F32),
            jax.ShapeDtypeStruct((1, depth // 16, width), F32),
            jax.ShapeDtypeStruct((1, depth // 16, width), F32),
        ),
        in_specs=[vmem_spec, vmem_spec],
        out_specs=(vmem_spec, vmem_spec, vmem_spec),
        compiler_params=pltpu.CompilerParams(vmem_limit_bytes=FINISH_BYTES),
        name="finish",
    )(fin, table)


def solution(mesh):
    in_specs = (P("client", None), P("client", None), P("client"), P("client"),
                P("cluster", None, None), P("cluster", None, None))
    out_specs = (P("client", None), P("cluster", "client", None), P("cluster", "client", None))
    return jax.shard_map(body, mesh=mesh, in_specs=in_specs, out_specs=out_specs, check_vma=False)
```

profile of v0, /device:TPU:8, one launch (start us, length us, event | category | flops | bytes accessed | tf_op | source)
XLA Modules:
  0.0 51.7 jit_solution(8642588712545218222)
XLA Ops:
  0.6 3.0 %picked.1 = (bf16[1536,512]{1,0:T(8,128)(2,1)S(1)}, bf16[1536,512]{1,0:T(8,128)(2,1)S(1)}, bf16[1536,256]{1,0:T(8,128)(2,1)S(1)}, bf16[1536,256]{1,0:T(8,128)(2,1)S(1)}) custom-call(bf16[1536,2048]{1,0:T(8,128)(2,1)} %uf.3, bf16[1536,2048]{1,0:T(8,128)(2,1)} %itf.3, s32[12,128]{1,0:T(8,128)} %bitcast.1, s32[16]{0:T(128)} %picks_hbm.1, ...), custom_call_target="tpu_custom_call" | custom-call | tf_op jit(solution)/shard_map/picked/pallas_call | solution.py:410
  3.6 47.3 %round.1 = (f32[2,128,512]{2,1,0:T(8,128)S(1)}, f32[2,8,1,128]{3,2,1,0:T(1,128)S(1)}) custom-call(bf16[1536,2048]{1,0:T(8,128)(2,1)} %uf.3, bf16[1536,2048]{1,0:T(8,128)(2,1)} %itf.3, s32[12,128]{1,0:T(8,128)} %bitcast.2, bf16[1,2048,512]{2,1,0:T(8,128)(2,1)} %uw.3, bf16[1,2048,512]{2,1,0:T(8,128)(2,1)} %iw.3, bf16[1536,512]{1,0:T(8,128)(2,1)S(1)} %get-tuple-element.9.us, ...), custom_call_target="tpu_custom_call" | custom-call | tf_op jit(solution)/shard_map/round/pallas_call | solution.py:425
  50.9 0.8 %finish.1 = (f32[16,16]{1,0:T(8,128)}, f32[1,128,512]{2,1,0:T(8,128)}, f32[1,128,512]{2,1,0:T(8,128)}) custom-call(f32[2,128,512]{2,1,0:T(8,128)S(1)} %get-tuple-element.13.fin, f32[2,8,1,128]{3,2,1,0:T(1,128)S(1)} %get-tuple-element.14.table), custom_call_target="tpu_custom_call" | custom-call | tf_op jit(solution)/shard_map/finish/pallas_call | solution.py:446
where the time goes:
time: 52 us; the launch traced here: 51.7 us
  Pallas kernels  51 us (98%)
  between operations  0.65 us (1%)
    pallas_call x1, Pallas kernels, body(): pl.pallas_call(functools.partial(kernel, (clients, rows, width, split, gr...  47.3 us
    pallas_call x1, Pallas kernels, body(): pl.pallas_call(functools.partial(picked, (clients, rows, width)), out_sha...  2.97 us

commit v1 on v0

--- a/solution.py
+++ b/solution.py
@@ -132,7 +132,7 @@
 def kernel(cfg, uf, itf, ids_hbm, uw, iw, us, its, cu, ci, fin, table,
            ids, fu, fi, wu, wi, iv, uvec, gt, crecv, ya, yb,
            xa1, xal, xar, xb1, xbl, xbr,
-           ld, cs, cr, ys, yr, xs, xr, ls, lr):
+           ld, cs, cr, ys, yr, xs, xr, ls, lr, up, down):
     clients, rows, width, split, groups, clusters = cfg
     total, depth = fu.shape
     per = clients // groups
@@ -182,26 +182,19 @@
         return pltpu.make_async_remote_copy(src_ref=src, dst_ref=dst, send_sem=ssem, recv_sem=rsem,
                                             device_id=peer, device_id_type=MESH)
 
-    def twin_copy():
-        return send(table.at[h, z], table.at[h, z], ls.at[0], lr.at[0], twin)
-
-    def loss_copy(n, up):
-        part = table.at[:, pl.ds((z + (nz - n if up else n)) % nz, 1)]
-        sem = 1 + 2 * n + (0 if up else 1)
-        return send(part, part, ls.at[sem], lr.at[sem], above if up else below)
-
-    def loss_copies(n):
-        return [loss_copy(n, True)] + ([loss_copy(n, False)] if n < nz // 2 - 1 else [])
-
-    def loss_step(n):
-        if n == 0:
-            twin_copy().wait_recv()
-        else:
-            for copy in loss_copies(n - 1):
-                copy.wait_recv()
+    def tell(n):
+        if n > 1:
+            pl.semaphore_wait(up.at[n - 1], 1)
+            if n <= nz // 2:
+                pl.semaphore_wait(down.at[n - 1], 1)
+        if n <= nz // 2:
+            pl.semaphore_signal(up.at[n], inc=1, device_id=above, device_id_type=MESH)
         if n < nz // 2:
-            for copy in loss_copies(n):
-                copy.start()
+            pl.semaphore_signal(down.at[n], inc=1, device_id=below, device_id_type=MESH)
+
+    def loss_copy(n):
+        mine = table.at[h, z]
+        return send(mine, mine, ls.at[n], lr.at[n], {"cluster": (k_me + n) % clusters})
 
     def core_copy(step, t):
         return send(gt.at[step, t, 1 - c], crecv.at[step, t], cs.at[step, t], cr.at[step, t], mate)
@@ -269,6 +262,7 @@
             gt[step, t, 1] = r[128:]
             if isinstance(step, int) and step == 0 and t == 0:
                 pl.semaphore_wait(barrier, 7)
+                tell(1)
             core_copy(step, t).start()
 
     def loaded(step):
@@ -327,6 +321,11 @@
             mean = jnp.sum(pair, axis=(0, 1), keepdims=True) * (1.0 / (rows * rows))
             losses = jnp.where(lane == g * per + n, mean, losses)
 
+        for m in range(groups):
+            @pl.when(g == m)
+            def _(m=m):
+                tell(m + 2)
+
         @pl.when(g == 0)
         def _():
             ya_arrived(2)
@@ -342,22 +341,19 @@
 
     losses = lax.fori_loop(0, groups, losses_of, jnp.zeros((1, 128), F32))
     table[h, z] = losses
-    twin_copy().start()
+    for n in range(1, clusters):
+        loss_copy(n).start()
     block(2 * NX - 1, (lambda: fu[:, columns(s_me, 2 * NX - 1)], lambda: fi[:, columns(s_me, 2 * NX - 1)]))
     ya_arrived(3)
     near_copy(2, 0, False).start()
-    loss_step(0)
     near_arrived(1)
     yb_copy(0).start()
     yb_copy(1).start()
     ready(2 * NX - 1)
-    loss_step(1)
     far_arrived(2, 0)
     far_arrived(2, 1)
     near_arrived(0)
     ya_arrived(0)
-    loss_step(2)
-    loss_step(3)
     for t in (0, 1):
         yb_copy(t).wait_recv()
         fin[t, split:, :] = gt[step_of(0, 0), t, c, split:, :] + yb[t]
@@ -365,12 +361,9 @@
         near_copy(2, t, True).wait_recv()
         near_copy(2, t, False).wait_recv()
         fin[t, :split, :] = gt[step_of(0, 0), t, c, :split, :] + xal[t] + xar[t]
-    loss_step(4)
-
-    twin_copy().wait_send()
-    for n in range(nz // 2):
-        for copy in loss_copies(n):
-            copy.wait_send()
+
+    for n in range(1, clusters):
+        loss_copy(n).wait()
     for step in range(2 * NX):
         for t in (0, 1):
             core_copy(step, t).wait_send()
@@ -438,6 +431,7 @@
             vmem((2, 2, rest, width), F32), vmem((2, 2, rest, width), F32), vmem((2, 2, rest, width), F32),
             dma((2 * NX + 1, 3)), dma((8, 2)), dma((8, 2)), dma((5, 2)), dma((5, 2)),
             dma((3, 3, 2)), dma((3, 3, 2)), dma((clusters,)), dma((clusters,)),
+            pltpu.SemaphoreType.REGULAR((5,)), pltpu.SemaphoreType.REGULAR((5,)),
         ],
         compiler_params=pltpu.CompilerParams(
             collective_id=0, has_side_effects=True, vmem_limit_bytes=ROUND_BYTES),

time: 52 us -> 47.1 us (0.906)
  Pallas kernels: 51 us -> 45.9 us
    pallas_call x1, Pallas kernels: 47.3 us -> 40.4 us  [body(): pl.pallas_call(functools.partial(kernel, (clients, rows, width, split, gr...]
    pallas_call x1, Pallas kernels: 2.97 us -> 4.67 us  [body(): pl.pallas_call(functools.partial(picked, (clients, rows, width)), out_sha...]
where the time goes in v1:
time: 47.1 us; the launch traced here: 46.5 us
  Pallas kernels  45.9 us (97%)
  between operations  0.65 us (1%)
    pallas_call x1, Pallas kernels, body(): pl.pallas_call(functools.partial(kernel, (clients, rows, width, split, gr...  40.4 us
    pallas_call x1, Pallas kernels, body(): pl.pallas_call(functools.partial(picked, (clients, rows, width)), out_sha...  4.67 us

profile of v1, /device:TPU:8, one launch (start us, length us, event | category | flops | bytes accessed | tf_op | source)
XLA Modules:
  0.0 46.5 jit_solution(5766529040137664634)
XLA Ops:
  0.6 4.7 %picked.1 = (bf16[1536,512]{1,0:T(8,128)(2,1)S(1)}, bf16[1536,512]{1,0:T(8,128)(2,1)S(1)}, bf16[1536,256]{1,0:T(8,128)(2,1)S(1)}, bf16[1536,256]{1,0:T(8,128)(2,1)S(1)}) custom-call(bf16[1536,2048]{1,0:T(8,128)(2,1)} %uf.3, bf16[1536,2048]{1,0:T(8,128)(2,1)} %itf.3, s32[12,128]{1,0:T(8,128)} %bitcast.1, s32[16]{0:T(128)} %picks_hbm.1, ...), custom_call_target="tpu_custom_call" | custom-call | tf_op jit(solution)/shard_map/picked/pallas_call | solution.py:403
  5.3 40.4 %round.1 = (f32[2,128,512]{2,1,0:T(8,128)S(1)}, f32[2,8,1,128]{3,2,1,0:T(1,128)S(1)}) custom-call(bf16[1536,2048]{1,0:T(8,128)(2,1)} %uf.3, bf16[1536,2048]{1,0:T(8,128)(2,1)} %itf.3, s32[12,128]{1,0:T(8,128)} %bitcast.2, bf16[1,2048,512]{2,1,0:T(8,128)(2,1)} %uw.3, bf16[1,2048,512]{2,1,0:T(8,128)(2,1)} %iw.3, bf16[1536,512]{1,0:T(8,128)(2,1)S(1)} %get-tuple-element.9.us, ...), custom_call_target="tpu_custom_call" | custom-call | tf_op jit(solution)/shard_map/round/pallas_call | solution.py:418
  45.7 0.8 %finish.1 = (f32[16,16]{1,0:T(8,128)}, f32[1,128,512]{2,1,0:T(8,128)}, f32[1,128,512]{2,1,0:T(8,128)}) custom-call(f32[2,128,512]{2,1,0:T(8,128)S(1)} %get-tuple-element.13.fin, f32[2,8,1,128]{3,2,1,0:T(1,128)S(1)} %get-tuple-element.14.table), custom_call_target="tpu_custom_call" | custom-call | tf_op jit(solution)/shard_map/finish/pallas_call | solution.py:440

commit v2 on v1

--- a/solution.py
+++ b/solution.py
@@ -153,10 +153,16 @@
     twin = {"cluster": (1 - h) * nz + z}
     above = {"cluster": h * nz + (z + 1) % nz}
     below = {"cluster": h * nz + (z + nz - 1) % nz}
+    has_above = z < nz - 1
+    has_below = z > 0
 
     barrier = pltpu.get_barrier_semaphore()
-    for peer in (mate, across, right, left, twin, above, below):
+    for peer in (mate, across, right, left, twin):
         pl.semaphore_signal(barrier, inc=1, device_id=peer, device_id_type=MESH)
+    for there, peer in ((has_above, above), (has_below, below)):
+        @pl.when(there)
+        def _(peer=peer):
+            pl.semaphore_signal(barrier, inc=1, device_id=peer, device_id_type=MESH)
 
     def feats(step, t):
         src, dst = ((uf, fu), (itf, fi))[t]
@@ -182,15 +188,23 @@
         return pltpu.make_async_remote_copy(src_ref=src, dst_ref=dst, send_sem=ssem, recv_sem=rsem,
                                             device_id=peer, device_id_type=MESH)
 
+    def pass_on(sem, has_source, has_target, target):
+        @pl.when(has_source)
+        def _():
+            pl.semaphore_wait(sem, 1)
+
+        @pl.when(has_target)
+        def _():
+            pl.semaphore_signal(sem, inc=1, device_id=target, device_id_type=MESH)
+
     def tell(n):
-        if n > 1:
-            pl.semaphore_wait(up.at[n - 1], 1)
-            if n <= nz // 2:
-                pl.semaphore_wait(down.at[n - 1], 1)
-        if n <= nz // 2:
-            pl.semaphore_signal(up.at[n], inc=1, device_id=above, device_id_type=MESH)
-        if n < nz // 2:
-            pl.semaphore_signal(down.at[n], inc=1, device_id=below, device_id_type=MESH)
+        @pl.when((z + 1) // 2 == n)
+        def _():
+            pass_on(up, has_below, has_above, above)
+
+        @pl.when((nz - z) // 2 == n)
+        def _():
+            pass_on(down, has_above, has_below, below)
 
     def loss_copy(n):
         mine = table.at[h, z]
@@ -240,20 +254,19 @@
             ya_copy(dx, t).wait_recv()
             add(own(dx, 0, t, A), ya.at[dx, t])
 
-    def ready(step):
+    def ready(step, t):
         dx, dy = ORDER[step // 2], 1 - step % 2
-        for t in (0, 1):
-            core_copy(step, t).wait_recv()
-            mine = gt.at[step, t, c]
-            mine[...] += crecv[step, t]
-            if dx == 2:
-                far_copy(dy, t).start()
-            if dy == 1:
-                ya_copy(dx, t).start()
-            if dx == 1 and t == 1:
-                near_copy(dy, 1, True).start()
-            if dx == 3 and t == 0:
-                near_copy(dy, 0, False).start()
+        core_copy(step, t).wait_recv()
+        mine = gt.at[step, t, c]
+        mine[...] += crecv[step, t]
+        if dx == 2:
+            far_copy(dy, t).start()
+        if dy == 1:
+            ya_copy(dx, t).start()
+        if dx == 1 and t == 1:
+            near_copy(dy, 1, True).start()
+        if dx == 3 and t == 0:
+            near_copy(dy, 0, False).start()
 
     def block(step, lhs):
         for t, (slope, feat) in enumerate(((us, lhs[0]), (its, lhs[1]))):
@@ -261,9 +274,15 @@
             gt[step, t, 0] = r[:128]
             gt[step, t, 1] = r[128:]
             if isinstance(step, int) and step == 0 and t == 0:
-                pl.semaphore_wait(barrier, 7)
-                tell(1)
+                ends = (z + nz - 2) // (nz - 1) + (2 * nz - 3 - z) // (nz - 1)
+                pl.semaphore_wait(barrier, 5 + ends)
+                tell(0)
             core_copy(step, t).start()
+            for n in range(2 * NX - 2):
+                if not isinstance(step, int):
+                    @pl.when(step == n + 1)
+                    def _(n=n, t=t):
+                        ready(n, t)
 
     def loaded(step):
         def of(t, buf):
@@ -285,18 +304,17 @@
                 feats(0, t).start()
 
         block(step, loaded(step))
-        for n in range(2 * NX - 2):
-            @pl.when(step == n + 1)
-            def _(n=n):
-                ready(n)
-                if n == 5:
-                    far_arrived(1, 0)
-                    far_arrived(1, 1)
+        @pl.when(step == 2 * NX - 2)
+        def _():
+            far_arrived(1, 0)
+            far_arrived(1, 1)
+
         return carry
 
     block(0, (lambda: cu[...], lambda: ci[...]))
     lax.fori_loop(1, 2 * NX - 1, blocks, 0)
-    ready(2 * NX - 2)
+    ready(2 * NX - 2, 0)
+    ready(2 * NX - 2, 1)
     far_arrived(0, 0)
     far_arrived(0, 1)
     for copy in rest_loads:
@@ -324,7 +342,7 @@
         for m in range(groups):
             @pl.when(g == m)
             def _(m=m):
-                tell(m + 2)
+                tell(m + 1)
 
         @pl.when(g == 0)
         def _():
@@ -349,7 +367,8 @@
     near_arrived(1)
     yb_copy(0).start()
     yb_copy(1).start()
-    ready(2 * NX - 1)
+    ready(2 * NX - 1, 0)
+    ready(2 * NX - 1, 1)
     far_arrived(2, 0)
     far_arrived(2, 1)
     near_arrived(0)
@@ -431,7 +450,7 @@
             vmem((2, 2, rest, width), F32), vmem((2, 2, rest, width), F32), vmem((2, 2, rest, width), F32),
             dma((2 * NX + 1, 3)), dma((8, 2)), dma((8, 2)), dma((5, 2)), dma((5, 2)),
             dma((3, 3, 2)), dma((3, 3, 2)), dma((clusters,)), dma((clusters,)),
-            pltpu.SemaphoreType.REGULAR((5,)), pltpu.SemaphoreType.REGULAR((5,)),
+            pltpu.SemaphoreType.REGULAR, pltpu.SemaphoreType.REGULAR,
         ],
         compiler_params=pltpu.CompilerParams(
             collective_id=0, has_side_effects=True, vmem_limit_bytes=ROUND_BYTES),

time: 47.1 us -> 46.1 us (0.979)
  the two profiles are of different devices: /device:TPU:8 before, /device:TPU:1 now
where the time goes in v2:
time: 46.1 us; the launch traced here: 45.6 us
  Pallas kernels  45 us (98%)
  between operations  0.65 us (1%)
    pallas_call x1, Pallas kernels, body(): pl.pallas_call(functools.partial(kernel, (clients, rows, width, split, gr...  39.3 us
    pallas_call x1, Pallas kernels, body(): pl.pallas_call(functools.partial(picked, (clients, rows, width)), out_sha...  4.84 us

profile of v2, /device:TPU:1, one launch (start us, length us, event | category | flops | bytes accessed | tf_op | source)
XLA Modules:
  0.0 45.6 jit_solution(12549493251554035532)
XLA Ops:
  0.6 4.8 %picked.1 = (bf16[1536,512]{1,0:T(8,128)(2,1)S(1)}, bf16[1536,512]{1,0:T(8,128)(2,1)S(1)}, bf16[1536,256]{1,0:T(8,128)(2,1)S(1)}, bf16[1536,256]{1,0:T(8,128)(2,1)S(1)}) custom-call(bf16[1536,2048]{1,0:T(8,128)(2,1)} %uf.3, bf16[1536,2048]{1,0:T(8,128)(2,1)} %itf.3, s32[12,128]{1,0:T(8,128)} %bitcast.1, s32[16]{0:T(128)} %picks_hbm.1, ...), custom_call_target="tpu_custom_call" | custom-call | tf_op jit(solution)/shard_map/picked/pallas_call | solution.py:422
  5.5 39.3 %round.1 = (f32[2,128,512]{2,1,0:T(8,128)S(1)}, f32[2,8,1,128]{3,2,1,0:T(1,128)S(1)}) custom-call(bf16[1536,2048]{1,0:T(8,128)(2,1)} %uf.3, bf16[1536,2048]{1,0:T(8,128)(2,1)} %itf.3, s32[12,128]{1,0:T(8,128)} %bitcast.2, bf16[1,2048,512]{2,1,0:T(8,128)(2,1)} %uw.3, bf16[1,2048,512]{2,1,0:T(8,128)(2,1)} %iw.3, bf16[1536,512]{1,0:T(8,128)(2,1)S(1)} %get-tuple-element.9.us, ...), custom_call_target="tpu_custom_call" | custom-call | tf_op jit(solution)/shard_map/round/pallas_call | solution.py:437
  44.8 0.8 %finish.1 = (f32[16,16]{1,0:T(8,128)}, f32[1,128,512]{2,1,0:T(8,128)}, f32[1,128,512]{2,1,0:T(8,128)}) custom-call(f32[2,128,512]{2,1,0:T(8,128)S(1)} %get-tuple-element.13.fin, f32[2,8,1,128]{3,2,1,0:T(1,128)S(1)} %get-tuple-element.14.table), custom_call_target="tpu_custom_call" | custom-call | tf_op jit(solution)/shard_map/finish/pallas_call | solution.py:459

commit v3 on v2

--- a/solution.py
+++ b/solution.py
@@ -10,7 +10,7 @@
 
 MESH = pl.DeviceIdType.MESH
 NX = 4
-ORDER = (2, 1, 3, 0)
+STEPS = ((2, 1), (2, 0), (1, 1), (3, 1), (1, 0), (3, 0), (0, 1), (0, 0))
 PAIR = 2
 PICKED_BYTES = 24 * 1024 * 1024
 ROUND_BYTES = 46 * 1024 * 1024
@@ -33,9 +33,10 @@
 
 
 def columns(s_me, step):
-    q = step // 2
-    dx = (2 + 3 * q + 3 * (q * (q - 1) // 2)) % NX
-    dy = 1 - step % 2
+    q = (step + 2) // 4
+    middle = q * (2 - q)
+    dx = (1 - q) * (2 - q) + middle * (1 + 2 * (step % 2))
+    dy = middle * (2 - step // 2) + (1 - middle) * (1 - step % 2)
     chip = ((s_me // 4 + dx) % NX) * 2 + ((s_me // 2) % 2 + dy) % 2
     return pl.ds(pl.multiple_of(chip * 256, 256), 256)
 
@@ -47,7 +48,7 @@
     k_me = lax.axis_index("cluster")
     loads = [pltpu.make_async_copy(src, dst, sem.at[n]) for n, (src, dst) in enumerate(
         ((picks_hbm, picks), (uw.at[0], wu), (iw.at[0], wi), (ids_hbm, ids)))]
-    for copy in loads:
+    for copy in loads[:2]:
         copy.start()
     loads[0].wait()
 
@@ -66,16 +67,24 @@
     def fetch(p):
         slot = p % 2
         copies = []
-        for n in range(PAIR):
-            at = pl.ds(pl.multiple_of(chosen[PAIR * p + n] * rows, rows), rows)
-            to = pl.ds(n * rows, rows)
-            copies.append(pltpu.make_async_copy(uf.at[at], bu.at[slot, to], bsem.at[slot, 0, n]))
-            copies.append(pltpu.make_async_copy(itf.at[at], bi.at[slot, to], bsem.at[slot, 1, n]))
+        for t, (src, dst) in enumerate(((uf, bu), (itf, bi))):
+            for n in range(PAIR):
+                at = pl.ds(pl.multiple_of(chosen[PAIR * p + n] * rows, rows), rows)
+                to = pl.ds(n * rows, rows)
+                copies.append(pltpu.make_async_copy(src.at[at], dst.at[slot, to], bsem.at[slot, t, n]))
         return copies
 
     @pl.when(pairs > 0)
     def _():
-        for copy in fetch(0):
+        for copy in fetch(0)[:PAIR]:
+            copy.start()
+
+    for copy in loads[2:]:
+        copy.start()
+
+    @pl.when(pairs > 0)
+    def _():
+        for copy in fetch(0)[PAIR:]:
             copy.start()
 
     def clear(n, carry):
@@ -87,27 +96,40 @@
     first = columns(lax.axis_index("client"), 0)
     ahead = [pltpu.make_async_copy(src.at[:, first], dst, sem.at[4 + t])
              for t, (src, dst) in enumerate(((uf, cu_out), (itf, ci_out)))]
-    for copy in ahead:
-        copy.start()
     lax.fori_loop(0, clients * rows // 64, clear, 0)
-    for copy in loads[1:]:
-        copy.wait()
+    loads[1].wait()
+
+    def rest():
+        for copy in loads[2:]:
+            copy.wait()
+        for copy in ahead:
+            copy.start()
+
+    @pl.when(pairs == 0)
+    def _():
+        rest()
 
     def pair(p, carry):
         slot = p % 2
-
-        @pl.when(p + 1 < pairs)
-        def _():
-            for copy in fetch(p + 1):
-                copy.start()
-
-        for copy in fetch(p):
+        for copy in fetch(p)[:PAIR]:
             copy.wait()
         pre = dot(bu[slot], wu[...])
         sig = 0.5 * jnp.tanh(0.5 * pre) + 0.5
         u = pre * sig
         uvec[...] = u.astype(BF16)
         dsilu[...] = sig + (u - u * sig)
+        for copy in fetch(p)[PAIR:]:
+            copy.wait()
+
+        @pl.when(p == 0)
+        def _():
+            rest()
+
+        @pl.when(p + 1 < pairs)
+        def _():
+            for copy in fetch(p + 1):
+                copy.start()
+
         iv[...] = dot(bi[slot], wi[...]).astype(BF16)
         for n in range(PAIR):
             client = chosen[PAIR * p + n]
@@ -179,7 +201,7 @@
     B = pl.ds(split, 128 - split)
 
     def step_of(dx, dy):
-        return 2 * ORDER.index(dx) + (1 - dy)
+        return STEPS.index((dx, dy))
 
     def own(dx, dy, t, part):
         return gt.at[step_of(dx, dy), t, c, part]
@@ -255,7 +277,7 @@
             add(own(dx, 0, t, A), ya.at[dx, t])
 
     def ready(step, t):
-        dx, dy = ORDER[step // 2], 1 - step % 2
+        dx, dy = STEPS[step]
         core_copy(step, t).wait_recv()
         mine = gt.at[step, t, c]
         mine[...] += crecv[step, t]
@@ -304,10 +326,11 @@
                 feats(0, t).start()
 
         block(step, loaded(step))
-        @pl.when(step == 2 * NX - 2)
-        def _():
-            far_arrived(1, 0)
-            far_arrived(1, 1)
+        for which in (1, 0):
+            @pl.when(step == 2 * NX - 2 - which)
+            def _(which=which):
+                far_arrived(which, 0)
+                far_arrived(which, 1)
 
         return carry
 
@@ -315,8 +338,6 @@
     lax.fori_loop(1, 2 * NX - 1, blocks, 0)
     ready(2 * NX - 2, 0)
     ready(2 * NX - 2, 1)
-    far_arrived(0, 0)
-    far_arrived(0, 1)
     for copy in rest_loads:
         copy.wait()
     for t in (0, 1):
@@ -361,12 +382,12 @@
     table[h, z] = losses
     for n in range(1, clusters):
         loss_copy(n).start()
-    block(2 * NX - 1, (lambda: fu[:, columns(s_me, 2 * NX - 1)], lambda: fi[:, columns(s_me, 2 * NX - 1)]))
-    ya_arrived(3)
-    near_copy(2, 0, False).start()
     near_arrived(1)
     yb_copy(0).start()
     yb_copy(1).start()
+    ya_arrived(3)
+    near_copy(2, 0, False).start()
+    block(2 * NX - 1, (lambda: fu[:, columns(s_me, 2 * NX - 1)], lambda: fi[:, columns(s_me, 2 * NX - 1)]))
     ready(2 * NX - 1, 0)
     ready(2 * NX - 1, 1)
     far_arrived(2, 0)

time: 46.1 us -> 46.3 us (level); the launches traced: 45.6 us -> 46.8 us
  Pallas kernels: 45 us -> 46.1 us
    pallas_call x1, Pallas kernels: 39.3 us -> 40 us  [body(): pl.pallas_call(functools.partial(kernel, (clients, rows, width, split, gr...]
where the time goes in v3:
time: 46.3 us; the launch traced here: 46.8 us
  Pallas kernels  46.1 us (100%)
  between operations  0.65 us (1%)
    pallas_call x1, Pallas kernels, body(): pl.pallas_call(functools.partial(kernel, (clients, rows, width, split, gr...  40 us
    pallas_call x1, Pallas kernels, body(): pl.pallas_call(functools.partial(picked, (clients, rows, width)), out_sha...  5.28 us

profile of v3, /device:TPU:1, one launch (start us, length us, event | category | flops | bytes accessed | tf_op | source)
XLA Modules:
  0.0 46.8 jit_solution(14366326764067881140)
XLA Ops:
  0.6 5.3 %picked.1 = (bf16[1536,512]{1,0:T(8,128)(2,1)S(1)}, bf16[1536,512]{1,0:T(8,128)(2,1)S(1)}, bf16[1536,256]{1,0:T(8,128)(2,1)S(1)}, bf16[1536,256]{1,0:T(8,128)(2,1)S(1)}) custom-call(bf16[1536,2048]{1,0:T(8,128)(2,1)} %uf.3, bf16[1536,2048]{1,0:T(8,128)(2,1)} %itf.3, s32[12,128]{1,0:T(8,128)} %bitcast.1, s32[16]{0:T(128)} %picks_hbm.1, ...), custom_call_target="tpu_custom_call" | custom-call | tf_op jit(solution)/shard_map/picked/pallas_call | solution.py:443
  5.9 40.0 %round.1 = (f32[2,128,512]{2,1,0:T(8,128)S(1)}, f32[2,8,1,128]{3,2,1,0:T(1,128)S(1)}) custom-call(bf16[1536,2048]{1,0:T(8,128)(2,1)} %uf.3, bf16[1536,2048]{1,0:T(8,128)(2,1)} %itf.3, s32[12,128]{1,0:T(8,128)} %bitcast.2, bf16[1,2048,512]{2,1,0:T(8,128)(2,1)} %uw.3, bf16[1,2048,512]{2,1,0:T(8,128)(2,1)} %iw.3, bf16[1536,512]{1,0:T(8,128)(2,1)S(1)} %get-tuple-element.9.us, ...), custom_call_target="tpu_custom_call" | custom-call | tf_op jit(solution)/shard_map/round/pallas_call | solution.py:458
  45.9 0.8 %finish.1 = (f32[16,16]{1,0:T(8,128)}, f32[1,128,512]{2,1,0:T(8,128)}, f32[1,128,512]{2,1,0:T(8,128)}) custom-call(f32[2,128,512]{2,1,0:T(8,128)S(1)} %get-tuple-element.13.fin, f32[2,8,1,128]{3,2,1,0:T(1,128)S(1)} %get-tuple-element.14.table), custom_call_target="tpu_custom_call" | custom-call | tf_op jit(solution)/shard_map/finish/pallas_call | solution.py:480

commit v4 on v2

--- a/solution.py
+++ b/solution.py
@@ -10,7 +10,7 @@
 
 MESH = pl.DeviceIdType.MESH
 NX = 4
-ORDER = (2, 1, 3, 0)
+STEPS = ((2, 1), (2, 0), (1, 1), (3, 1), (1, 0), (3, 0), (0, 1), (0, 0))
 PAIR = 2
 PICKED_BYTES = 24 * 1024 * 1024
 ROUND_BYTES = 46 * 1024 * 1024
@@ -33,9 +33,10 @@
 
 
 def columns(s_me, step):
-    q = step // 2
-    dx = (2 + 3 * q + 3 * (q * (q - 1) // 2)) % NX
-    dy = 1 - step % 2
+    q = (step + 2) // 4
+    middle = q * (2 - q)
+    dx = (1 - q) * (2 - q) + middle * (1 + 2 * (step % 2))
+    dy = middle * (2 - step // 2) + (1 - middle) * (1 - step % 2)
     chip = ((s_me // 4 + dx) % NX) * 2 + ((s_me // 2) % 2 + dy) % 2
     return pl.ds(pl.multiple_of(chip * 256, 256), 256)
 
@@ -179,7 +180,7 @@
     B = pl.ds(split, 128 - split)
 
     def step_of(dx, dy):
-        return 2 * ORDER.index(dx) + (1 - dy)
+        return STEPS.index((dx, dy))
 
     def own(dx, dy, t, part):
         return gt.at[step_of(dx, dy), t, c, part]
@@ -255,7 +256,7 @@
             add(own(dx, 0, t, A), ya.at[dx, t])
 
     def ready(step, t):
-        dx, dy = ORDER[step // 2], 1 - step % 2
+        dx, dy = STEPS[step]
         core_copy(step, t).wait_recv()
         mine = gt.at[step, t, c]
         mine[...] += crecv[step, t]
@@ -304,10 +305,11 @@
                 feats(0, t).start()
 
         block(step, loaded(step))
-        @pl.when(step == 2 * NX - 2)
-        def _():
-            far_arrived(1, 0)
-            far_arrived(1, 1)
+        for which in (1, 0):
+            @pl.when(step == 2 * NX - 2 - which)
+            def _(which=which):
+                far_arrived(which, 0)
+                far_arrived(which, 1)
 
         return carry
 
@@ -315,8 +317,6 @@
     lax.fori_loop(1, 2 * NX - 1, blocks, 0)
     ready(2 * NX - 2, 0)
     ready(2 * NX - 2, 1)
-    far_arrived(0, 0)
-    far_arrived(0, 1)
     for copy in rest_loads:
         copy.wait()
     for t in (0, 1):
@@ -361,12 +361,12 @@
     table[h, z] = losses
     for n in range(1, clusters):
         loss_copy(n).start()
-    block(2 * NX - 1, (lambda: fu[:, columns(s_me, 2 * NX - 1)], lambda: fi[:, columns(s_me, 2 * NX - 1)]))
-    ya_arrived(3)
-    near_copy(2, 0, False).start()
     near_arrived(1)
     yb_copy(0).start()
     yb_copy(1).start()
+    ya_arrived(3)
+    near_copy(2, 0, False).start()
+    block(2 * NX - 1, (lambda: fu[:, columns(s_me, 2 * NX - 1)], lambda: fi[:, columns(s_me, 2 * NX - 1)]))
     ready(2 * NX - 1, 0)
     ready(2 * NX - 1, 1)
     far_arrived(2, 0)

time: 46.1 us -> 45.7 us (level)
  Pallas kernels: 45 us -> 44.1 us
    pallas_call x1, Pallas kernels: 39.3 us -> 38.6 us  [body(): pl.pallas_call(functools.partial(kernel, (clients, rows, width, split, gr...]
where the time goes in v4:
time: 45.7 us; the launch traced here: 44.8 us
  Pallas kernels  44.1 us (96%)
  between operations  0.65 us (1%)
    pallas_call x1, Pallas kernels, body(): pl.pallas_call(functools.partial(kernel, (clients, rows, width, split, gr...  38.6 us
    pallas_call x1, Pallas kernels, body(): pl.pallas_call(functools.partial(picked, (clients, rows, width)), out_sha...  4.67 us

profile of v4, /device:TPU:1, one launch (start us, length us, event | category | flops | bytes accessed | tf_op | source)
XLA Modules:
  0.0 44.8 jit_solution(16144772785308064624)
XLA Ops:
  0.6 4.7 %picked.1 = (bf16[1536,512]{1,0:T(8,128)(2,1)S(1)}, bf16[1536,512]{1,0:T(8,128)(2,1)S(1)}, bf16[1536,256]{1,0:T(8,128)(2,1)S(1)}, bf16[1536,256]{1,0:T(8,128)(2,1)S(1)}) custom-call(bf16[1536,2048]{1,0:T(8,128)(2,1)} %uf.3, bf16[1536,2048]{1,0:T(8,128)(2,1)} %itf.3, s32[12,128]{1,0:T(8,128)} %bitcast.1, s32[16]{0:T(128)} %picks_hbm.1, ...), custom_call_target="tpu_custom_call" | custom-call | tf_op jit(solution)/shard_map/picked/pallas_call | solution.py:422
  5.3 38.6 %round.1 = (f32[2,128,512]{2,1,0:T(8,128)S(1)}, f32[2,8,1,128]{3,2,1,0:T(1,128)S(1)}) custom-call(bf16[1536,2048]{1,0:T(8,128)(2,1)} %uf.3, bf16[1536,2048]{1,0:T(8,128)(2,1)} %itf.3, s32[12,128]{1,0:T(8,128)} %bitcast.2, bf16[1,2048,512]{2,1,0:T(8,128)(2,1)} %uw.3, bf16[1,2048,512]{2,1,0:T(8,128)(2,1)} %iw.3, bf16[1536,512]{1,0:T(8,128)(2,1)S(1)} %get-tuple-element.9.us, ...), custom_call_target="tpu_custom_call" | custom-call | tf_op jit(solution)/shard_map/round/pallas_call | solution.py:437
  44.0 0.8 %finish.1 = (f32[16,16]{1,0:T(8,128)}, f32[1,128,512]{2,1,0:T(8,128)}, f32[1,128,512]{2,1,0:T(8,128)}) custom-call(f32[2,128,512]{2,1,0:T(8,128)S(1)} %get-tuple-element.13.fin, f32[2,8,1,128]{3,2,1,0:T(1,128)S(1)} %get-tuple-element.14.table), custom_call_target="tpu_custom_call" | custom-call | tf_op jit(solution)/shard_map/finish/pallas_call | solution.py:459
